TPU v7x, 128 devices: a whole 4x4x4 slice. The times are simulated.
128 devices in a mesh: rows: 16 (over y, z), seq: 8 (over x, core).
Axes of the slice: x: 4, y: 4, z: 4, core: 2. Of those that a mesh axis runs over, the one named last changes fastest.
Arguments:
- residual_in: bfloat16 [16, 2048, 3200], P('rows', 'seq'), may hold values from -6 to 6
- norm_gain: float32 [3200], replicated, may hold values from 0.1 to 1.9
- qkv_weight: bfloat16 [3200, 6144], P(None, 'seq')
- qk_gain: float32 [2, 2048], P(None, 'seq')
- out_weight: bfloat16 [2048, 3200], P('seq'), may hold values from -0.125 to 0.125
- layer_scale: float32 [3200], replicated, may hold values from 1 to 6
- segment_ids: int32 [16, 2048], P('rows', 'seq'), may hold values from 0 to 2, as said below
- pad_mask: int32 [16, 2048], P('rows', 'seq'), may hold values from 0 to 1, as said below
- ln_weight: float32 [12800], replicated, may hold values from 0.1 to 1.9
- ln_bias: float32 [12800], replicated, may hold values from -3 to 3
- fc_weight: bfloat16 [12800, 6144], P('rows'), may hold values from -0.0546875 to 0.0546875
- fc_bias: float32 [6144], replicated, may hold values from -3 to 3
- owner: int32 [16], replicated, may hold values from 0 to 15, each once
Outputs:
- features: bfloat16 [16, 512, 6144], P('rows', 'seq')
Inputs may be any that keep to these rules, and one draw needn't show every extreme that they name: `segment_ids`: within a row, segment ids never fall and change only at multiples of 1024 tokens; picture tokens carry ids below 2, padding tokens carry 2 and stand at the end of the row; the first tile is never padding. pad_mask is 0 exactly where segment_ids equals 2. `owner`: each index of rows owns exactly one row.
All inputs are finite; a program needn't handle non-finite values.
Results may differ from a plain program's by a relative error of at most 0.025.
Values may be sent and summed in bfloat16 or wider, within the bound.
A program may use at most 128 MiB of HBM per device.

v0:
```python
import jax
import jax.numpy as jnp
from jax import lax
from jax.sharding import PartitionSpec as P

D = 3200
HEAD_DIM = 128
HEADS = 16
GRID = 32
MASK_SHIFT = 1000000.0


def attend_dense(query_norm, key_norm, value_half, row_segments, block_len, scale):
    length, heads_here = (query_norm.shape[0], query_norm.shape[1])
    block_count = length // block_len

    def one_block(packed):
        query_block, query_seg = packed
        scores = (
            jnp.einsum("qhd,khd->hqk", query_block, key_norm, preferred_element_type=jnp.float32)
            * scale
        )
        same_seg = (query_seg[:, None] == row_segments[None, :])[None]
        scores = jnp.where(same_seg, scores, -1e30)
        peak_val = jnp.max(scores, axis=-1, keepdims=True)
        exp_terms = jnp.exp(scores - peak_val)
        probs = (exp_terms / jnp.sum(exp_terms, axis=-1, keepdims=True)).astype(jnp.bfloat16)
        return jnp.einsum(
            "hqk,khd->qhd", probs, value_half, preferred_element_type=jnp.float32
        ).astype(jnp.bfloat16)

    blocks_out = lax.map(
        one_block,
        (
            query_norm.reshape(block_count, block_len, heads_here, HEAD_DIM),
            row_segments.reshape(block_count, block_len),
        ),
    )
    return blocks_out.reshape(length, heads_here * HEAD_DIM)


def per_device(
    residual_in,
    norm_gain,
    qkv_weight,
    qk_gain,
    out_weight,
    layer_scale,
    segment_ids,
    pad_mask,
    ln_weight,
    ln_bias,
    fc_weight,
    fc_bias,
    owner,
):
    seq_count = lax.axis_size("seq")
    seq_me = lax.axis_index("seq")
    tokens = residual_in[0].astype(jnp.float32)
    shard_rows = tokens.shape[0]
    normed = (
        tokens * lax.rsqrt(jnp.mean(tokens * tokens, axis=-1, keepdims=True) + 1e-06) * norm_gain
    ).astype(jnp.bfloat16)
    row_tokens = lax.all_gather(normed, "seq", axis=0, tiled=True)
    length = row_tokens.shape[0]
    heads_here = qkv_weight.shape[1] // (3 * HEAD_DIM)
    projected = jnp.dot(row_tokens, qkv_weight, preferred_element_type=jnp.float32).reshape(
        length, heads_here, 3, HEAD_DIM
    )
    query_raw = projected[:, :, 0]
    key_raw = projected[:, :, 1]
    value_half = projected[:, :, 2].astype(jnp.bfloat16)
    seg_spread = lax.dynamic_update_slice_in_dim(
        jnp.zeros((length,), jnp.float32),
        segment_ids[0].astype(jnp.float32),
        seq_me * shard_rows,
        0,
    )
    stats = lax.psum(
        jnp.stack(
            [
                jnp.sum(query_raw * query_raw, axis=(1, 2)),
                jnp.sum(key_raw * key_raw, axis=(1, 2)),
                seg_spread,
            ]
        ),
        "seq",
    )
    query_sq, key_sq, row_segments = (stats[0], stats[1], stats[2])
    norm_width = HEADS * HEAD_DIM
    gain_pair = qk_gain.reshape(2, heads_here, HEAD_DIM)
    query_norm = (
        query_raw * lax.rsqrt(query_sq / norm_width + 1e-06)[:, None, None] * gain_pair[0]
    ).astype(jnp.bfloat16)
    key_norm = (
        key_raw * lax.rsqrt(key_sq / norm_width + 1e-06)[:, None, None] * gain_pair[1]
    ).astype(jnp.bfloat16)
    block_len = min(512, length)
    scale = HEAD_DIM ** (-0.5)
    attended = attend_dense(query_norm, key_norm, value_half, row_segments, block_len, scale)
    group_width = attended.shape[1]
    own_heads = lax.all_to_all(attended.reshape(seq_count, shard_rows, group_width), "seq", 0, 0)
    full_out_weight = lax.all_gather(out_weight, "seq", axis=0, tiled=False)
    group_terms = jnp.einsum(
        "gtc,gcd->gtd", own_heads, full_out_weight, preferred_element_type=jnp.float32
    ).astype(jnp.bfloat16)
    attn = jnp.sum(group_terms.astype(jnp.float32), axis=0)
    hidden = tokens + layer_scale * attn
    half_grid = GRID // 2
    lines = shard_rows // (2 * GRID)
    merged_count = shard_rows // 4
    merged = jnp.transpose(hidden.reshape(lines, 2, half_grid, 2, D), (0, 2, 1, 3, 4)).reshape(
        merged_count, 4 * D
    )
    centre = merged - jnp.mean(merged, axis=-1, keepdims=True)
    spread = jnp.mean(centre * centre, axis=-1, keepdims=True)
    merged_norm = (centre * lax.rsqrt(spread + 1e-05) * ln_weight + ln_bias).astype(jnp.bfloat16)
    merged_mask = (
        pad_mask[0]
        .reshape(lines, 2, half_grid, 2)[:, 0, :, 0]
        .reshape(merged_count)
        .astype(jnp.float32)
    )
    row_count = lax.axis_size("rows")
    row_me = lax.axis_index("rows")
    slabs = lax.all_to_all(merged_norm, "rows", split_axis=1, concat_axis=0, tiled=True)
    owner_hot = (owner[None, :] == jnp.arange(row_count, dtype=jnp.int32)[:, None]).astype(
        jnp.bfloat16
    )
    ordered = jnp.einsum(
        "jp,pms->jms",
        owner_hot,
        slabs.reshape(row_count, merged_count, -1),
        preferred_element_type=jnp.float32,
    ).astype(jnp.bfloat16)
    ordered = ordered.reshape(row_count * merged_count, -1)
    partial = jnp.dot(ordered, fc_weight, preferred_element_type=jnp.float32).reshape(
        row_count, merged_count, -1
    )
    own_slot = (jnp.arange(row_count, dtype=jnp.int32) == owner[row_me]).astype(jnp.float32)
    shift = own_slot[:, None] * ((merged_mask - 1.0) * MASK_SHIFT)[None, :]
    partial = (partial + shift[:, :, None]).astype(jnp.bfloat16)
    summed = lax.psum_scatter(
        partial.reshape(row_count * merged_count, -1), "rows", scatter_dimension=0, tiled=True
    ).astype(jnp.float32)
    result = jax.nn.gelu(summed + fc_bias, approximate=False)
    return result.astype(jnp.bfloat16)[None]


def solution(mesh):
    return jax.shard_map(
        per_device,
        mesh=mesh,
        in_specs=(
            P("rows", "seq", None),
            P(),
            P(None, "seq"),
            P(None, "seq"),
            P("seq", None),
            P(),
            P("rows", "seq"),
            P("rows", "seq"),
            P(),
            P(),
            P("rows", None),
            P(),
            P(),
        ),
        out_specs=P("rows", "seq", None),
        check_vma=False,
    )
```

profile of v0, /device:TPU:1, one launch (start us, length us, event | category | flops | bytes accessed | tf_op | source)
XLA Modules:
  0.0 404.6 jit_solution(10836090393352335551)
XLA Ops:
  11.7 72.5 %all-gather.4.cloned.1.call-done = bf16[2048,3200]{1,0:T(8,128)(2,1)} async-done(((bf16[256,3200]{1,0:T(8,128)(2,1)}), bf16[2048,3200]{1,0:T(8,128)(2,1)}) %all-gather.4.cloned.1.call-update) | async-done | bytes 13107216 | tf_op jit(solution)/shard_map/all_gather | solution.py:64
  84.2 15.7 %fusion.74 = f32[2048,768]{0,1:T(8,128)S(1)} fusion(bf16[2048,3200]{1,0:T(8,128)(2,1)} %all-gather.4.cloned.1.call-done, bf16[3200,768]{1,0:T(8,128)(2,1)} %param.17), kind=kOutput, calls=%fused_computation.97 | convolution fusion | flops 10066329600 | bytes 24313856 | tf_op jit(solution)/shard_map/dot_general | solution.py:67
  109.3 22.6 %psum.7 = f32[3,2048]{1,0:T(4,128)S(1)} all-reduce(f32[3,2048]{1,0:T(4,128)S(1)} %pad_maximum_fusion), channel_id=1, replica_groups=mesh['rows'=16,'seq'=8] {'seq'}, use_global_device_ids=true, to_apply=%region_3.0 | all-reduce | flops 6144 | bytes 49152 | tf_op jit(solution)/shard_map/psum | solution.py:79
  133.3 3.0 multiply_convert_fusion
  137.6 53.7 %while.10 = (s32[]{:T(128)}, bf16[4,512,2,128]{3,2,1,0:T(2,128)(2,1)S(1)}, f32[4,512]{1,0:T(4,128)S(1)}, f32[1,2048]{1,0:T(1,128)S(1)}, bf16[4,512,2,128]{3,1,0,...) while((s32[]{:T(128)}, ...), condition=%wide.region_7.8_spmd, body=%wide.region_4.7_spmd.sunk | while | flops 1087506432 | bytes 26237560 | solution.py:32
  138.3 7.8 %fusion.90 = (f32[2,512]{1,0:T(2,128)S(1)}, f32[2,512,2048]{2,1,0:T(8,128)}) fusion(pred[512,2048]{1,0:T(8,128)(4,1)S(1)} %broadcast_compare_fusion.2, bf16[2048,2,128]{2,0,1:T(8,128)(2,1)} %get-tuple-element.158, bf16[4,512,2,128]{3,1,0,2:T(8,128)(2,1)} %get-tuple-element.157, s32[]{:T(128)} %get-tuple-element.145), kind=kOutput, calls=%fused_computation.94.clone.1 | convolution fusion | flops 545261568 | bytes 10752512 | tf_op jit(solution)/shard_map/while/body/eval_jaxpr/sub | solution.py:26
  146.1 4.7 %fusion.91 = bf16[1,512,2,128]{3,1,2,0:T(8,128)(2,1)S(1)} fusion(bf16[2048,2,128]{2,0,1:T(8,128)(2,1)S(1)} %copy-done.5, f32[2,512,2048]{2,1,0:T(8,128)} %get-tuple-element.135, f32[2,512]{1,0:T(2,128)S(1)} %get-tuple-element.136), kind=kOutput, calls=%fused_computation.11.clone.1 | convolution fusion | flops 541196288 | bytes 9703424 | tf_op jit(solution)/shard_map/while/body/eval_jaxpr/hqk,khd->qhd/dot_general | solution.py:28
  151.8 7.7 %fusion.90 = (f32[2,512]{1,0:T(2,128)S(1)}, f32[2,512,2048]{2,1,0:T(8,128)}) fusion(pred[512,2048]{1,0:T(8,128)(4,1)S(1)} %broadcast_compare_fusion.2, bf16[2048,2,128]{2,0,1:T(8,128)(2,1)} %get-tuple-element.158, bf16[4,512,2,128]{3,1,0,2:T(8,128)(2,1)} %get-tuple-element.157, s32[]{:T(128)} %get-tuple-element.145), kind=kOutput, calls=%fused_computation.94.clone.1 | convolution fusion | flops 545261568 | bytes 10752512 | tf_op jit(solution)/shard_map/while/body/eval_jaxpr/sub | solution.py:26
  159.5 4.7 %fusion.91 = bf16[1,512,2,128]{3,1,2,0:T(8,128)(2,1)S(1)} fusion(bf16[2048,2,128]{2,0,1:T(8,128)(2,1)S(1)} %copy-done.5, f32[2,512,2048]{2,1,0:T(8,128)} %get-tuple-element.135, f32[2,512]{1,0:T(2,128)S(1)} %get-tuple-element.136), kind=kOutput, calls=%fused_computation.11.clone.1 | convolution fusion | flops 541196288 | bytes 9703424 | tf_op jit(solution)/shard_map/while/body/eval_jaxpr/hqk,khd->qhd/dot_general | solution.py:28
  165.2 7.7 %fusion.90 = (f32[2,512]{1,0:T(2,128)S(1)}, f32[2,512,2048]{2,1,0:T(8,128)}) fusion(pred[512,2048]{1,0:T(8,128)(4,1)S(1)} %broadcast_compare_fusion.2, bf16[2048,2,128]{2,0,1:T(8,128)(2,1)} %get-tuple-element.158, bf16[4,512,2,128]{3,1,0,2:T(8,128)(2,1)} %get-tuple-element.157, s32[]{:T(128)} %get-tuple-element.145), kind=kOutput, calls=%fused_computation.94.clone.1 | convolution fusion | flops 545261568 | bytes 10752512 | tf_op jit(solution)/shard_map/while/body/eval_jaxpr/sub | solution.py:26
  172.9 4.7 %fusion.91 = bf16[1,512,2,128]{3,1,2,0:T(8,128)(2,1)S(1)} fusion(bf16[2048,2,128]{2,0,1:T(8,128)(2,1)S(1)} %copy-done.5, f32[2,512,2048]{2,1,0:T(8,128)} %get-tuple-element.135, f32[2,512]{1,0:T(2,128)S(1)} %get-tuple-element.136), kind=kOutput, calls=%fused_computation.11.clone.1 | convolution fusion | flops 541196288 | bytes 9703424 | tf_op jit(solution)/shard_map/while/body/eval_jaxpr/hqk,khd->qhd/dot_general | solution.py:28
  178.6 7.7 %fusion.90 = (f32[2,512]{1,0:T(2,128)S(1)}, f32[2,512,2048]{2,1,0:T(8,128)}) fusion(pred[512,2048]{1,0:T(8,128)(4,1)S(1)} %broadcast_compare_fusion.2, bf16[2048,2,128]{2,0,1:T(8,128)(2,1)} %get-tuple-element.158, bf16[4,512,2,128]{3,1,0,2:T(8,128)(2,1)} %get-tuple-element.157, s32[]{:T(128)} %get-tuple-element.145), kind=kOutput, calls=%fused_computation.94.clone.1 | convolution fusion | flops 545261568 | bytes 10752512 | tf_op jit(solution)/shard_map/while/body/eval_jaxpr/sub | solution.py:26
  186.3 4.7 %fusion.91 = bf16[1,512,2,128]{3,1,2,0:T(8,128)(2,1)S(1)} fusion(bf16[2048,2,128]{2,0,1:T(8,128)(2,1)S(1)} %copy-done.5, f32[2,512,2048]{2,1,0:T(8,128)} %get-tuple-element.135, f32[2,512]{1,0:T(2,128)S(1)} %get-tuple-element.136), kind=kOutput, calls=%fused_computation.11.clone.1 | convolution fusion | flops 541196288 | bytes 9703424 | tf_op jit(solution)/shard_map/while/body/eval_jaxpr/hqk,khd->qhd/dot_general | solution.py:28
  192.8 7.8 %all-to-all-start = ((bf16[8,256,256]{2,1,0:T(8,128)(2,1)}), bf16[8,256,256]{2,1,0:T(8,128)(2,1)S(1)}, u32[]{:S(2)}, u32[]{:S(2)}) async-start(bf16[8,256,256]{2,1,0:T(8,128)(2,1)} %reshape_reshape.3), calls=%async_computation | async-start | bytes 2097152 | tf_op jit(solution)/shard_map/all_to_all | solution.py:102
  203.7 12.1 %all-to-all-done = bf16[8,256,256]{2,1,0:T(8,128)(2,1)S(1)} async-done(((bf16[8,256,256]{2,1,0:T(8,128)(2,1)}), bf16[8,256,256]{2,1,0:T(8,128)(2,1)S(1)}, u32[]{:S(2)}, u32[]{:S(2)}) %all-to-all-start) | async-done | bytes 1048608 | tf_op jit(solution)/shard_map/all_to_all | solution.py:102
  215.7 10.6 %convert_reduce_fusion = f32[256,3200]{1,0:T(8,128)} fusion(bf16[8,256,256]{2,1,0:T(8,128)(2,1)S(1)} %all-to-all-done, bf16[8,256,3200]{2,1,0:T(8,128)(2,1)} %bitcast.99), kind=kOutput, calls=%fused_computation.24 | convolution fusion | flops 3374284800 | bytes 17432576 | tf_op jit(solution)/shard_map/gtc,gcd->gtd/dot_general | solution.py:104
  226.3 5.3 %reduce_sum.69 = f32[4,2,16,2,3200]{4,3,2,1,0:T(2,128)} reshape(f32[256,3200]{1,0:T(8,128)} %convert_reduce_fusion) | data formatting | bytes 6553600 | tf_op jit(solution)/shard_map/reduce_sum | solution.py:107
  231.7 4.2 %fusion.66 = (f32[4,16]{1,0:T(4,128)S(1)}, f32[4,16,2,2,3200]{4,3,1,2,0:T(2,128)S(1)}) fusion(f32[4,2,16,2,3200]{4,3,2,1,0:T(2,128)S(1)} %copy-done.3, f32[4,2,16,2,3200]{4,3,2,1,0:T(2,128)} %reduce_sum.69, f32[3200]{0:T(1024)S(1)} %copy-done.9), kind=kLoop, calls=%fused_computation.93 | loop fusion | flops 2457536 | bytes 9843456 | tf_op jit(solution)/shard_map/reduce_sum | solution.py:115
  238.3 4.5 %reshape.212 = f32[64,16,800]{2,1,0:T(8,128)} reshape(f32[4,16,2,2,3200]{4,3,2,1,0:T(2,128)S(1)} %copy.36) | data formatting | bytes 6553600 | tf_op jit(solution)/shard_map/reshape | solution.py:112
  247.1 7.0 %all-to-all-start.1 = ((bf16[64,16,800]{2,0,1:T(8,128)(2,1)}), bf16[64,16,800]{2,0,1:T(8,128)(2,1)S(1)}, u32[]{:S(2)}, u32[]{:S(2)}) async-start(bf16[64,16,800]{2,0,1:T(8,128)(2,1)} %copy.37), calls=%async_computation.1 | async-start | bytes 3670016 | tf_op jit(solution)/shard_map/all_to_all | solution.py:126
  257.0 20.2 %all-to-all-done.1 = bf16[64,16,800]{2,0,1:T(8,128)(2,1)S(1)} async-done(((bf16[64,16,800]{2,0,1:T(8,128)(2,1)}), bf16[64,16,800]{2,0,1:T(8,128)(2,1)S(1)}, u32[]{:S(2)}, u32[]{:S(2)}) %all-to-all-start.1) | async-done | bytes 1638432 | tf_op jit(solution)/shard_map/all_to_all | solution.py:126
  278.5 19.2 %add_convert_fusion = bf16[16,64,6144]{2,1,0:T(8,128)(2,1)} fusion(f32[16,64]{1,0:T(8,128)S(1)} %broadcast_multiply_fusion, bf16[800,6144]{1,0:T(8,128)(2,1)} %param.25, bf16[16,64,800]{2,0,1:T(8,128)(2,1)S(1)} %fusion.38), kind=kOutput, calls=%fused_computation.25 | convolution fusion | flops 10078912512 | bytes 24055808 | tf_op jit(solution)/shard_map/dot_general | solution.py:137
  297.8 95.1 %reduce-scatter.2.cloned.1.call-done = bf16[64,6144]{1,0:T(8,128)(2,1)} async-done(((bf16[1024,6144]{1,0:T(8,128)(2,1)}), bf16[64,6144]{1,0:T(8,128)(2,1)}) %reduce-scatter.2.cloned.1.call-update) | async-done | bytes 786448 | tf_op jit(solution)/shard_map/reduce_scatter | solution.py:143
  392.9 5.2 %fusion.54 = bf16[1,64,6144]{2,1,0:T(8,128)(2,1)} fusion(bf16[64,6144]{1,0:T(8,128)(2,1)} %reduce-scatter.2.cloned.1.call-done, f32[6144]{0:T(1024)S(1)} %copy-done.8), kind=kLoop, calls=%fused_computation.70 | loop fusion | flops 26345472 | bytes 1597440 | tf_op jit(solution)/shard_map/broadcast_in_dim | solution.py:147
  (93 shorter events, 36.5 us)
Async XLA Ops:
  6.5 2.0 copy-start.1
  6.5 77.7 %all-gather.4.cloned.1.call-start = ((), (), s32[]{:S(2)}) async-start(), calls=%async_computation.3 | async-start | bytes 14745600 | tf_op jit(solution)/shard_map/all_gather | solution.py:64
  10.9 0.8 copy-start.11
  10.9 0.8 copy-start.10
  10.9 192.8 %all-gather.6.cloned.1.call-start = ((), (), s32[]{:S(2)}) async-start(), calls=%async_computation.5 | async-start | bytes 14745600 | tf_op jit(solution)/shard_map/all_gather | solution.py:103
  107.3 1.6 copy-start
  136.3 1.3 copy-start.4
  138.3 7.8 %copy-start.5 = (bf16[2048,2,128]{2,0,1:T(8,128)(2,1)S(1)}, bf16[2048,2,128]{2,0,1:T(8,128)(2,1)}, u32[]{:S(2)}) copy-start(bf16[2048,2,128]{2,0,1:T(8,128)(2,1)} %get-tuple-element.159) | copy-start | bytes 3145732 | tf_op jit(solution)/shard_map/while
  151.7 7.8 %copy-start.5 = (bf16[2048,2,128]{2,0,1:T(8,128)(2,1)S(1)}, bf16[2048,2,128]{2,0,1:T(8,128)(2,1)}, u32[]{:S(2)}) copy-start(bf16[2048,2,128]{2,0,1:T(8,128)(2,1)} %get-tuple-element.159) | copy-start | bytes 3145732 | tf_op jit(solution)/shard_map/while
  165.2 7.8 %copy-start.5 = (bf16[2048,2,128]{2,0,1:T(8,128)(2,1)S(1)}, bf16[2048,2,128]{2,0,1:T(8,128)(2,1)}, u32[]{:S(2)}) copy-start(bf16[2048,2,128]{2,0,1:T(8,128)(2,1)} %get-tuple-element.159) | copy-start | bytes 3145732 | tf_op jit(solution)/shard_map/while
  178.6 7.8 %copy-start.5 = (bf16[2048,2,128]{2,0,1:T(8,128)(2,1)S(1)}, bf16[2048,2,128]{2,0,1:T(8,128)(2,1)}, u32[]{:S(2)}) copy-start(bf16[2048,2,128]{2,0,1:T(8,128)(2,1)} %get-tuple-element.159) | copy-start | bytes 3145732 | tf_op jit(solution)/shard_map/while
  191.3 9.3 %copy-start.2 = (bf16[1,256,3200]{2,1,0:T(8,128)(2,1)S(1)}, bf16[1,256,3200]{2,1,0:T(8,128)(2,1)}, u32[]{:S(2)}) copy-start(bf16[1,256,3200]{2,1,0:T(8,128)(2,1)} %param.15) | copy-start | bytes 4915204
  192.8 22.9 %all-to-all-start = ((bf16[8,256,256]{2,1,0:T(8,128)(2,1)}), bf16[8,256,256]{2,1,0:T(8,128)(2,1)S(1)}, u32[]{:S(2)}, u32[]{:S(2)}) async-start(bf16[8,256,256]{2,1,0:T(8,128)(2,1)} %reshape_reshape.3), calls=%async_computation | async-start | bytes 2097152 | tf_op jit(solution)/shard_map/all_to_all | solution.py:102
  200.6 2.8 copy-start.6
  200.6 2.9 copy-start.7
  226.3 5.3 %copy-start.3 = (f32[4,2,16,2,3200]{4,3,2,1,0:T(2,128)S(1)}, f32[4,2,16,2,3200]{4,3,2,1,0:T(2,128)}, u32[]{:S(2)}) copy-start(f32[4,2,16,2,3200]{4,3,2,1,0:T(2,128)} %reshape.214) | copy-start | bytes 9830404
  226.3 5.3 %copy-start.9 = (f32[3200]{0:T(1024)S(1)}, f32[3200]{0:T(1024)}, u32[]{:S(2)}) copy-start(f32[3200]{0:T(1024)} %param.20) | copy-start | bytes 38404
  247.1 7.6 %copy-start.12 = (s32[1,256]{1,0:T(1,128)S(1)}, s32[1,256]{1,0:T(1,128)}, u32[]{:S(2)}) copy-start(s32[1,256]{1,0:T(1,128)} %param.22) | copy-start | bytes 3076
  247.1 8.6 %copy-start.13 = (s32[16]{0:T(128)S(1)}, s32[16]{0:T(128)}, u32[]{:S(2)}) copy-start(s32[16]{0:T(128)} %param.27) | copy-start | bytes 196
  247.1 30.1 %all-to-all-start.1 = ((bf16[64,16,800]{2,0,1:T(8,128)(2,1)}), bf16[64,16,800]{2,0,1:T(8,128)(2,1)S(1)}, u32[]{:S(2)}, u32[]{:S(2)}) async-start(bf16[64,16,800]{2,0,1:T(8,128)(2,1)} %copy.37), calls=%async_computation.1 | async-start | bytes 3670016 | tf_op jit(solution)/shard_map/all_to_all | solution.py:126
  254.2 138.7 %reduce-scatter.2.cloned.1.call-start = ((), (), s32[]{:S(2)}) async-start(), calls=%async_computation.4 | async-start | bytes 13369344 | tf_op jit(solution)/shard_map/reduce_scatter | solution.py:143
  297.7 95.1 %copy-start.8 = (f32[6144]{0:T(1024)S(1)}, f32[6144]{0:T(1024)}, u32[]{:S(2)}) copy-start(f32[6144]{0:T(1024)} %param.26) | copy-start | bytes 73732
Sparse Core Ops, SparseCore 0:
  11.0 73.1 all-gather.3
  85.9 70.2 all-gather.5
  297.9 94.9 reduce-scatter.1
where the time goes:
time: 405 us
  waiting for transfers between devices  201 us (50%)
  matrix products  96.5 us (24%)
  local copies, waits for them, and re-layouts  29 us (7%)
  other arithmetic  27.6 us (7%)
  blocking collectives  22.6 us (6%)
  starting transfers between devices  14.9 us (4%)
  between operations  13.3 us (3%)
    reduce_scatter x1, waiting for transfers between devices, per_device(): lax.psum_scatter(partial.reshape(row_count * merged_count, -1), 'rows', s...  95.1 us
    all_gather x1, waiting for transfers between devices, per_device(): row_tokens = lax.all_gather(normed, 'seq', axis=0, tiled=True)  72.5 us
    sub x4, matrix products, one_block(): exp_terms = jnp.exp(scores - peak_val)  31 us
    psum x1, blocking collectives, per_device(): lax.psum(jnp.stack([jnp.sum(query_raw * query_raw, axis=(1, 2)), jnp.sum(...  22.6 us
    all_to_all x1, waiting for transfers between devices, per_device(): lax.all_to_all(merged_norm, 'rows', split_axis=1, concat_axis=0, tiled=True)  20.2 us
    dot_general x1, matrix products, per_device(): jnp.dot(ordered, fc_weight, preferred_element_type=jnp.float32)  19.2 us
    dot_general x4, matrix products, one_block(): jnp.einsum('hqk,khd->qhd', probs, value_half, preferred_element_type=jnp....  18.7 us
    dot_general x1, matrix products, per_device(): jnp.dot(row_tokens, qkv_weight, preferred_element_type=jnp.float32)  15.7 us
  transfers between devices with their start and end apart: 5, of which 4 were waited for; matrix products, arithmetic and copies ran while one was open for 22% of the time, Pallas kernels for 0%

commit v1 on v0

--- a/solution.py
+++ b/solution.py
@@ -61,7 +61,10 @@
     normed = (
         tokens * lax.rsqrt(jnp.mean(tokens * tokens, axis=-1, keepdims=True) + 1e-06) * norm_gain
     ).astype(jnp.bfloat16)
-    row_tokens = lax.all_gather(normed, "seq", axis=0, tiled=True)
+    big = lax.psum(1, axis_name="seq")
+    aux = jnp.stack(big * [normed], axis=0)
+    frame_out = lax.all_to_all(aux, "seq", 0, 0)
+    row_tokens = jnp.concatenate(frame_out, axis=0)
     length = row_tokens.shape[0]
     heads_here = qkv_weight.shape[1] // (3 * HEAD_DIM)
     projected = jnp.dot(row_tokens, qkv_weight, preferred_element_type=jnp.float32).reshape(

time: 405 us -> 541 us (1.34)
  waiting for transfers between devices: 201 us -> 317 us
  local copies, waits for them, and re-layouts: 29 us -> 40.3 us
  starting transfers between devices: 14.9 us -> 21.7 us
    all_to_all x0 -> x1, waiting for transfers between devices: none -> 189 us  [per_device(): frame_out = lax.all_to_all(aux, 'seq', 0, 0)]
    all_gather x1 -> x0, waiting for transfers between devices: 72.5 us -> none  [per_device(): row_tokens = lax.all_gather(normed, 'seq', axis=0, tiled=True)]
    all_to_all x0 -> x1, starting transfers between devices: none -> 6.68 us  [per_device(): frame_out = lax.all_to_all(aux, 'seq', 0, 0)]
    another operation x0 -> x1, local copies, waits for them, and re-layouts: none -> 6.38 us  [per_device(): aux = jnp.stack(big * [normed], axis=0)]
  transfers between devices with their start and end apart: 5 -> 5, of which waited for: 4 -> 4; matrix products, arithmetic and copies ran while one was open for 22% -> 18% of each run, Pallas kernels for 0% -> 0%
where the time goes in v1:
time: 541 us; the launch traced here: 540 us
  waiting for transfers between devices  317 us (59%)
  matrix products  96.4 us (18%)
  local copies, waits for them, and re-layouts  40.3 us (7%)
  other arithmetic  29.6 us (5%)
  starting transfers between devices  21.7 us (4%)
  blocking collectives  21.2 us (4%)
  between operations  13.6 us (3%)
    all_to_all x1, waiting for transfers between devices, per_device(): frame_out = lax.all_to_all(aux, 'seq', 0, 0)  189 us
    reduce_scatter x1, waiting for transfers between devices, per_device(): lax.psum_scatter(partial.reshape(row_count * merged_count, -1), 'rows', s...  95 us
    sub x4, matrix products, one_block(): exp_terms = jnp.exp(scores - peak_val)  30.6 us
    psum x1, blocking collectives, per_device(): lax.psum(jnp.stack([jnp.sum(query_raw * query_raw, axis=(1, 2)), jnp.sum(...  21.2 us
    all_to_all x1, waiting for transfers between devices, per_device(): lax.all_to_all(merged_norm, 'rows', split_axis=1, concat_axis=0, tiled=True)  20.2 us
    dot_general x4, matrix products, one_block(): jnp.einsum('hqk,khd->qhd', probs, value_half, preferred_element_type=jnp....  19.6 us
    dot_general x1, matrix products, per_device(): jnp.dot(ordered, fc_weight, preferred_element_type=jnp.float32)  19.2 us
    dot_general x1, matrix products, per_device(): jnp.dot(row_tokens, qkv_weight, preferred_element_type=jnp.float32)  15.1 us
  transfers between devices with their start and end apart: 5, of which 4 were waited for; matrix products, arithmetic and copies ran while one was open for 18% of the time, Pallas kernels for 0%

profile of v1, /device:TPU:1, one launch (start us, length us, event | category | flops | bytes accessed | tf_op | source)
XLA Modules:
  0.0 539.7 jit_solution(16324315204737987439)
XLA Ops:
  9.7 6.4 %stack.11 = bf16[8,256,3200]{2,1,0:T(8,128)(2,1)} broadcast(bf16[256,3200]{1,0:T(8,128)(2,1)S(1)} %fusion.37), dimensions={1,2} | broadcast | bytes 14745600 | tf_op jit(solution)/shard_map/stack | solution.py:65
  16.1 6.7 %all-to-all-start = ((bf16[8,256,3200]{2,1,0:T(8,128)(2,1)}), bf16[8,256,3200]{2,1,0:T(8,128)(2,1)}, u32[]{:S(2)}, u32[]{:S(2)}) async-start(bf16[8,256,3200]{2,1,0:T(8,128)(2,1)} %stack.11), calls=%async_computation | async-start | bytes 26214400 | tf_op jit(solution)/shard_map/all_to_all | solution.py:66
  23.5 7.5 %copy.27 = bf16[3200,768]{0,1:T(8,128)(2,1)} copy(bf16[3200,768]{1,0:T(8,128)(2,1)} %param.17) | data formatting | bytes 9830400 | tf_op args[2]
  31.1 188.8 %all-to-all-done = bf16[8,256,3200]{2,1,0:T(8,128)(2,1)} async-done(((bf16[8,256,3200]{2,1,0:T(8,128)(2,1)}), bf16[8,256,3200]{2,1,0:T(8,128)(2,1)}, u32[]{:S(2)}, u32[]{:S(2)}) %all-to-all-start) | async-done | bytes 13107232 | tf_op jit(solution)/shard_map/all_to_all | solution.py:66
  219.9 15.1 %fusion.72 = f32[2048,2,3,128]{3,0,2,1:T(8,128)S(1)} fusion(bf16[2048,3200,1,1]{1,0,3,2:T(8,128)(2,1)} %bitcast.9, bf16[2,3,128,3200]{3,2,1,0:T(8,128)(2,1)} %bitcast.83), kind=kOutput, calls=%fused_computation.96 | convolution fusion | flops 10066329600 | bytes 24313856 | tf_op jit(solution)/shard_map/dot_general | solution.py:70
  238.3 21.2 %psum.7 = f32[3,2048]{1,0:T(4,128)S(1)} all-reduce(f32[3,2048]{1,0:T(4,128)S(1)} %pad_maximum_fusion), channel_id=1, replica_groups=mesh['rows'=16,'seq'=8] {'seq'}, use_global_device_ids=true, to_apply=%region_3.0 | all-reduce | flops 6144 | bytes 49152 | tf_op jit(solution)/shard_map/psum | solution.py:82
  268.1 56.9 %while.10 = (s32[]{:T(128)}, bf16[4,512,2,128]{3,2,1,0:T(2,128)(2,1)}, f32[4,512]{1,0:T(4,128)S(1)}, f32[1,2048]{1,0:T(1,128)S(1)}, bf16[4,512,2,128]{3,1,2,0:T(...) while((s32[]{:T(128)}, bf16[4,512,2,128]{3,2,1,0:T(2,128)(2,1)}, ...), condition=%wide.region_7.8_spmd, body=%wide.region_4.7_spmd.sunk | while | flops 1087506432 | bytes 22043736 | solution.py:32
  268.8 7.7 %fusion.88 = (f32[2,512]{1,0:T(2,128)S(1)}, f32[2,512,2048]{2,1,0:T(8,128)}) fusion(pred[512,2048]{1,0:T(8,128)(4,1)S(1)} %broadcast_compare_fusion.2, bf16[2048,2,128]{2,0,1:T(8,128)(2,1)} %get-tuple-element.137, bf16[4,512,2,128]{3,1,2,0:T(8,128)(2,1)} %get-tuple-element.136, s32[]{:T(128)} %get-tuple-element.124), kind=kOutput, calls=%fused_computation.93.clone.1 | convolution fusion | flops 545261568 | bytes 10752512 | tf_op jit(solution)/shard_map/while/body/eval_jaxpr/sub | solution.py:26
  276.5 4.9 fusion.89
  283.0 7.7 %fusion.88 = (f32[2,512]{1,0:T(2,128)S(1)}, f32[2,512,2048]{2,1,0:T(8,128)}) fusion(pred[512,2048]{1,0:T(8,128)(4,1)S(1)} %broadcast_compare_fusion.2, bf16[2048,2,128]{2,0,1:T(8,128)(2,1)} %get-tuple-element.137, bf16[4,512,2,128]{3,1,2,0:T(8,128)(2,1)} %get-tuple-element.136, s32[]{:T(128)} %get-tuple-element.124), kind=kOutput, calls=%fused_computation.93.clone.1 | convolution fusion | flops 545261568 | bytes 10752512 | tf_op jit(solution)/shard_map/while/body/eval_jaxpr/sub | solution.py:26
  290.7 4.9 fusion.89
  297.3 7.7 %fusion.88 = (f32[2,512]{1,0:T(2,128)S(1)}, f32[2,512,2048]{2,1,0:T(8,128)}) fusion(pred[512,2048]{1,0:T(8,128)(4,1)S(1)} %broadcast_compare_fusion.2, bf16[2048,2,128]{2,0,1:T(8,128)(2,1)} %get-tuple-element.137, bf16[4,512,2,128]{3,1,2,0:T(8,128)(2,1)} %get-tuple-element.136, s32[]{:T(128)} %get-tuple-element.124), kind=kOutput, calls=%fused_computation.93.clone.1 | convolution fusion | flops 545261568 | bytes 10752512 | tf_op jit(solution)/shard_map/while/body/eval_jaxpr/sub | solution.py:26
  304.9 4.9 fusion.89
  311.5 7.7 %fusion.88 = (f32[2,512]{1,0:T(2,128)S(1)}, f32[2,512,2048]{2,1,0:T(8,128)}) fusion(pred[512,2048]{1,0:T(8,128)(4,1)S(1)} %broadcast_compare_fusion.2, bf16[2048,2,128]{2,0,1:T(8,128)(2,1)} %get-tuple-element.137, bf16[4,512,2,128]{3,1,2,0:T(8,128)(2,1)} %get-tuple-element.136, s32[]{:T(128)} %get-tuple-element.124), kind=kOutput, calls=%fused_computation.93.clone.1 | convolution fusion | flops 545261568 | bytes 10752512 | tf_op jit(solution)/shard_map/while/body/eval_jaxpr/sub | solution.py:26
  319.1 4.9 fusion.89
  327.5 7.0 %all-to-all-start.1 = ((bf16[8,256,256]{2,1,0:T(8,128)(2,1)}), bf16[8,256,256]{2,1,0:T(8,128)(2,1)S(1)}, u32[]{:S(2)}, u32[]{:S(2)}) async-start(bf16[8,256,256]{2,1,0:T(8,128)(2,1)} %reshape_reshape.3), calls=%async_computation.1 | async-start | bytes 2097152 | tf_op jit(solution)/shard_map/all_to_all | solution.py:105
  337.6 12.1 %all-to-all-done.1 = bf16[8,256,256]{2,1,0:T(8,128)(2,1)S(1)} async-done(((bf16[8,256,256]{2,1,0:T(8,128)(2,1)}), bf16[8,256,256]{2,1,0:T(8,128)(2,1)S(1)}, u32[]{:S(2)}, u32[]{:S(2)}) %all-to-all-start.1) | async-done | bytes 1048608 | tf_op jit(solution)/shard_map/all_to_all | solution.py:105
  349.7 10.6 %convert_reduce_fusion = f32[256,3200]{1,0:T(8,128)} fusion(bf16[8,256,256]{2,1,0:T(8,128)(2,1)S(1)} %all-to-all-done.1, bf16[8,256,3200]{2,1,0:T(8,128)(2,1)} %bitcast.91), kind=kOutput, calls=%fused_computation.24 | convolution fusion | flops 3374284800 | bytes 17432576 | tf_op jit(solution)/shard_map/gtc,gcd->gtd/dot_general | solution.py:107
  360.2 5.3 reduce_sum.69
  381.1 8.0 %all-to-all-start.2 = ((bf16[64,16,800]{2,0,1:T(8,128)(2,1)}), bf16[64,16,800]{2,0,1:T(8,128)(2,1)S(1)}, u32[]{:S(2)}, u32[]{:S(2)}) async-start(bf16[64,16,800]{2,0,1:T(8,128)(2,1)} %copy.31), calls=%async_computation.2 | async-start | bytes 3670016 | tf_op jit(solution)/shard_map/all_to_all | solution.py:129
  391.9 20.2 %all-to-all-done.2 = bf16[64,16,800]{2,0,1:T(8,128)(2,1)S(1)} async-done(((bf16[64,16,800]{2,0,1:T(8,128)(2,1)}), bf16[64,16,800]{2,0,1:T(8,128)(2,1)S(1)}, u32[]{:S(2)}, u32[]{:S(2)}) %all-to-all-start.2) | async-done | bytes 1638432 | tf_op jit(solution)/shard_map/all_to_all | solution.py:129
  413.4 19.2 %add_convert_fusion = bf16[16,64,6144]{2,1,0:T(8,128)(2,1)} fusion(f32[16,64]{1,0:T(8,128)S(1)} %broadcast_multiply_fusion, bf16[800,6144]{1,0:T(8,128)(2,1)} %param.25, bf16[16,64,800]{2,0,1:T(8,128)(2,1)S(1)} %fusion.34), kind=kOutput, calls=%fused_computation.25 | convolution fusion | flops 10078912512 | bytes 24055808 | tf_op jit(solution)/shard_map/dot_general | solution.py:140
  432.7 95.0 %reduce-scatter.2.cloned.1.call-done = bf16[64,6144]{1,0:T(8,128)(2,1)} async-done(((bf16[1024,6144]{1,0:T(8,128)(2,1)}), bf16[64,6144]{1,0:T(8,128)(2,1)}) %reduce-scatter.2.cloned.1.call-update) | async-done | bytes 786448 | tf_op jit(solution)/shard_map/reduce_scatter | solution.py:146
  527.6 5.2 fusion.52
  (78 shorter events, 47.5 us)
Async XLA Ops:
  6.5 2.0 copy-start
  16.1 203.8 %all-to-all-start = ((bf16[8,256,3200]{2,1,0:T(8,128)(2,1)}), bf16[8,256,3200]{2,1,0:T(8,128)(2,1)}, u32[]{:S(2)}, u32[]{:S(2)}) async-start(bf16[8,256,3200]{2,1,0:T(8,128)(2,1)} %stack.11), calls=%async_computation | async-start | bytes 26214400 | tf_op jit(solution)/shard_map/all_to_all | solution.py:66
  22.8 326.9 %all-gather.3.cloned.1.call-start = ((), (), s32[]{:S(2)}) async-start(), calls=%async_computation.5 | async-start | bytes 14745600 | tf_op jit(solution)/shard_map/all_gather | solution.py:106
  23.5 7.5 %copy-start.8 = (s32[1,256]{1,0:T(1,128)S(1)}, s32[1,256]{1,0:T(1,128)}, u32[]{:S(2)}) copy-start(s32[1,256]{1,0:T(1,128)} %param.21) | copy-start | bytes 3076
  23.5 7.5 %copy-start.7 = (f32[2,256]{1,0:T(2,128)S(1)}, f32[2,256]{1,0:T(2,128)}, u32[]{:S(2)}) copy-start(f32[2,256]{1,0:T(2,128)} %param.18) | copy-start | bytes 6148
  235.0 3.3 copy-start.2
  327.5 22.1 %all-to-all-start.1 = ((bf16[8,256,256]{2,1,0:T(8,128)(2,1)}), bf16[8,256,256]{2,1,0:T(8,128)(2,1)S(1)}, u32[]{:S(2)}, u32[]{:S(2)}) async-start(bf16[8,256,256]{2,1,0:T(8,128)(2,1)} %reshape_reshape.3), calls=%async_computation.1 | async-start | bytes 2097152 | tf_op jit(solution)/shard_map/all_to_all | solution.py:105
  334.5 2.8 copy-start.3
  334.5 2.9 copy-start.4
  360.2 5.3 copy-start.1
  360.2 5.3 copy-start.6
  381.1 8.6 %copy-start.9 = (s32[1,256]{1,0:T(1,128)S(1)}, s32[1,256]{1,0:T(1,128)}, u32[]{:S(2)}) copy-start(s32[1,256]{1,0:T(1,128)} %param.22) | copy-start | bytes 3076
  381.1 9.6 %copy-start.10 = (s32[16]{0:T(128)S(1)}, s32[16]{0:T(128)}, u32[]{:S(2)}) copy-start(s32[16]{0:T(128)} %param.27) | copy-start | bytes 196
  381.1 31.0 %all-to-all-start.2 = ((bf16[64,16,800]{2,0,1:T(8,128)(2,1)}), bf16[64,16,800]{2,0,1:T(8,128)(2,1)S(1)}, u32[]{:S(2)}, u32[]{:S(2)}) async-start(bf16[64,16,800]{2,0,1:T(8,128)(2,1)} %copy.31), calls=%async_computation.2 | async-start | bytes 3670016 | tf_op jit(solution)/shard_map/all_to_all | solution.py:129
  389.1 138.6 %reduce-scatter.2.cloned.1.call-start = ((), (), s32[]{:S(2)}) async-start(), calls=%async_computation.4 | async-start | bytes 13369344 | tf_op jit(solution)/shard_map/reduce_scatter | solution.py:146
  432.6 95.0 %copy-start.5 = (f32[6144]{0:T(1024)S(1)}, f32[6144]{0:T(1024)}, u32[]{:S(2)}) copy-start(f32[6144]{0:T(1024)} %param.26) | copy-start | bytes 73732
Sparse Core Ops, SparseCore 0:
  25.3 141.7 all-gather.2
  432.8 94.8 reduce-scatter.1
